TPU v7x, 32 devices: a whole 2x2x4 slice. The times are simulated.
32 devices in a mesh: dp: 8 (over z, x), tensor: 4 (over y, core).
Axes of the slice: x: 2, y: 2, z: 4, core: 2. Of those that a mesh axis runs over, the one named last changes fastest.
Arguments:
- tokens: bfloat16 [25088, 768], P(('dp', 'tensor')), may hold values from -6 to 6
- cotangent: bfloat16 [25088, 768], P(('dp', 'tensor')), may hold values from -6 to 6
- block_patches: int32 [32], P('dp'), may hold values from 196 to 784, as said below
- qkv_weight: bfloat16 [3, 768, 768], P(None, 'dp', 'tensor'), may hold values from -0.21875 to 0.21875
- out_weight: bfloat16 [768, 768], P('tensor', 'dp'), may hold values from -0.875 to 0.875
- up_weight: bfloat16 [768, 3072], P('dp', 'tensor'), may hold values from -0.21875 to 0.21875
- down_weight: bfloat16 [3072, 768], P('tensor', 'dp'), may hold values from -0.109375 to 0.109375
- vectors: float32 [9216], replicated, may hold values from -0.7 to 1.7, as said below
- momentum: float32 [1], replicated, may hold values from 0.4 to 0.7
- target_qkv: float32 [3, 768, 768], P(None, 'dp', 'tensor'), may hold values from -0.21875 to 0.21875
- target_out: float32 [768, 768], P('tensor', 'dp'), may hold values from -0.875 to 0.875
- target_up: float32 [768, 3072], P('dp', 'tensor'), may hold values from -0.21875 to 0.21875
- target_down: float32 [3072, 768], P('tensor', 'dp'), may hold values from -0.109375 to 0.109375
- target_vectors: float32 [9216], replicated, may hold values from -0.7 to 1.7, as said below
Outputs:
- output: bfloat16 [25088, 768], P(('dp', 'tensor'))
- grad_tokens: bfloat16 [25088, 768], P(('dp', 'tensor'))
- grad_qkv: float32 [3, 768, 768], P(None, 'dp', 'tensor')
- grad_out: float32 [768, 768], P('tensor', 'dp')
- grad_up: float32 [768, 3072], P('dp', 'tensor')
- grad_down: float32 [3072, 768], P('tensor', 'dp')
- grad_vectors: float32 [9216], replicated
- next_qkv: float32 [3, 768, 768], P(None, 'dp', 'tensor')
- next_out: float32 [768, 768], P('tensor', 'dp')
- next_up: float32 [768, 3072], P('dp', 'tensor')
- next_down: float32 [3072, 768], P('tensor', 'dp')
- next_vectors: float32 [9216], replicated
Inputs may be any that keep to these rules, and one draw needn't show every extreme that they name: `block_patches`: each block of 784 rows holds either one image of 784 patches (entry 784) or four images of 196 patches, one after another (entry 196); both kinds occur in every draw. `vectors`: the gains (the first and third pieces of 768) lie between 0.3 and 1.7. `target_vectors`: laid out as vectors, with gains between 0.3 and 1.7.
All inputs are finite; a program needn't handle non-finite values.
Results may differ from a plain program's by a relative error of at most 0.012.
Values may be sent and summed in bfloat16 or wider, within the bound.
A program may use at most 192 MiB of HBM per device.

v0:
```python
import jax
import jax.numpy as jnp
from jax import lax
from jax.sharding import PartitionSpec as P

HD = 64
BOTH = ("dp", "tensor")
F32 = jnp.float32
BF16 = jnp.bfloat16


def unpack(vectors, d, ff):
    cuts = [d * i for i in range(8)] + [7 * d + ff, 8 * d + ff]
    return tuple((vectors[a:b] for a, b in zip(cuts[:-1], cuts[1:])))


def norm_parts(values):
    centred = values - jnp.mean(values, axis=-1, keepdims=True)
    inverse = lax.rsqrt(jnp.mean(centred * centred, axis=-1, keepdims=True) + 1e-06)
    return (centred * inverse, inverse)


def norm_backward(grad_normed, scaled, inverse, gain):
    weighted = grad_normed * gain
    return inverse * (
        weighted
        - jnp.mean(weighted, axis=-1, keepdims=True)
        - scaled * jnp.mean(weighted * scaled, axis=-1, keepdims=True)
    )


def gelu_parts(v):
    cdf = 0.5 * (1.0 + lax.erf(v * 0.5**0.5))
    return (v * cdf, cdf + v * jnp.exp(-0.5 * v * v) * (2.0 * jnp.pi) ** (-0.5))


def dot(a, b, dims):
    return lax.dot_general(a, b, (dims, ((), ())), preferred_element_type=F32)


def pack_shards(qkv, out, up, down):
    first = jnp.concatenate([qkv[0], qkv[1], qkv[2], out.T], axis=1)
    return jnp.stack([first, up, down.T])


def gather_blocks(shards, dp, tensor):
    every = lax.all_gather(shards, BOTH, axis=0)
    b, r, c = shards.shape
    every = every.reshape(dp, tensor, b, r, c).transpose(2, 1, 0, 3, 4)
    return every.reshape(b, tensor, dp * r, c)


def scatter_blocks(blocks, dp, tensor):
    b, t, rows, c = blocks.shape
    r = rows // dp
    pieces = blocks.reshape(b, tensor, dp, r, c).transpose(2, 1, 0, 3, 4)
    pieces = pieces.reshape(dp * tensor, b, r, c)
    return lax.psum_scatter(pieces, BOTH, scatter_dimension=0, tiled=True)[0]


def local_layer(tokens, cotangent, patches, blocks, vectors):
    rows, d = tokens.shape
    tensor, c = (blocks.shape[1], blocks.shape[3])
    w = c // 4
    ff = tensor * c
    heads = d // HD
    gain1, bias1, gain2, bias2, bias_q, bias_v, bias_out, bias_up, bias_down = unpack(
        vectors, d, ff
    )
    first, up, downt = (blocks[0], blocks[1], blocks[2])
    factor = HD ** (-0.5)
    x = tokens.astype(F32)
    scaled1, inverse1 = norm_parts(x)
    normed1 = (scaled1 * gain1 + bias1).astype(BF16)
    mixed = jnp.einsum("rd,tdc->rtc", normed1, first[:, :, : 3 * w], preferred_element_type=F32)
    query = (mixed[:, :, :w].reshape(rows, d) + bias_q).astype(BF16).reshape(rows, heads, HD)
    key = mixed[:, :, w : 2 * w].reshape(rows, d).astype(BF16).reshape(rows, heads, HD)
    value = (mixed[:, :, 2 * w :].reshape(rows, d) + bias_v).astype(BF16).reshape(rows, heads, HD)
    images = jnp.arange(rows, dtype=jnp.int32) // patches
    allowed = images[:, None] == images[None, :]
    scores = jnp.einsum("qhd,khd->hqk", query, key, preferred_element_type=F32) * factor
    scores = jnp.where(allowed[None], scores, -1e30)
    raised = jnp.exp(scores - jnp.max(scores, axis=-1, keepdims=True))
    soft = raised / jnp.sum(raised, axis=-1, keepdims=True)
    soft_low = soft.astype(BF16)
    attended = jnp.einsum("hqk,khd->qhd", soft_low, value, preferred_element_type=F32).astype(BF16)
    flat = attended.reshape(rows, tensor, w)
    outt = first[:, :, 3 * w :]
    residual = x + jnp.einsum("rte,tde->rd", flat, outt, preferred_element_type=F32) + bias_out
    scaled2, inverse2 = norm_parts(residual)
    normed2 = (scaled2 * gain2 + bias2).astype(BF16)
    pre = jnp.einsum("rd,tdf->rtf", normed2, up, preferred_element_type=F32) + bias_up.reshape(
        tensor, c
    )
    active, slope = gelu_parts(pre)
    active = active.astype(BF16)
    second = jnp.einsum("rtf,tdf->rd", active, downt, preferred_element_type=F32)
    output = (residual + second + bias_down).astype(BF16)
    grad_active = jnp.einsum("rd,tdf->rtf", cotangent, downt, preferred_element_type=F32)
    grad_pre = (grad_active * slope).astype(BF16)
    g_down = jnp.einsum("rd,rtf->tdf", cotangent, active, preferred_element_type=F32)
    g_up = jnp.einsum("rd,rtf->tdf", normed2, grad_pre, preferred_element_type=F32)
    grad_normed2 = jnp.einsum("rtf,tdf->rd", grad_pre, up, preferred_element_type=F32)
    grad_result = cotangent.astype(F32)
    grad_residual = grad_result + norm_backward(grad_normed2, scaled2, inverse2, gain2)
    grad_branch = grad_residual.astype(BF16)
    g_outt = jnp.einsum("rd,rte->tde", grad_branch, flat, preferred_element_type=F32)
    grad_att = jnp.einsum("rd,tde->rte", grad_branch, outt, preferred_element_type=F32)
    grad_att = grad_att.astype(BF16).reshape(rows, heads, HD)
    grad_value = jnp.einsum("hqk,qhd->khd", soft_low, grad_att, preferred_element_type=F32)
    grad_soft = jnp.einsum("qhd,khd->hqk", grad_att, value, preferred_element_type=F32)
    grad_scores = (soft * (grad_soft - jnp.sum(soft * grad_soft, axis=-1, keepdims=True))).astype(
        BF16
    )
    grad_query = jnp.einsum("hqk,khd->qhd", grad_scores, key, preferred_element_type=F32) * factor
    grad_key = jnp.einsum("hqk,qhd->khd", grad_scores, query, preferred_element_type=F32) * factor
    three = [g.astype(BF16).reshape(rows, tensor, w) for g in (grad_query, grad_key, grad_value)]
    grad_mixed = jnp.concatenate(three, axis=2)
    g_qkv = jnp.einsum("rd,rtc->tdc", normed1, grad_mixed, preferred_element_type=F32)
    grad_normed1 = jnp.einsum(
        "rtc,tdc->rd", grad_mixed, first[:, :, : 3 * w], preferred_element_type=F32
    )
    grad_tokens = (grad_residual + norm_backward(grad_normed1, scaled1, inverse1, gain1)).astype(
        BF16
    )
    grads = jnp.stack(
        [
            jnp.concatenate([g_qkv, g_outt], axis=2).astype(BF16),
            g_up.astype(BF16),
            g_down.astype(BF16),
        ]
    )

    def total(values):
        return jnp.sum(values.astype(F32), axis=0).reshape(-1)

    sums = jnp.concatenate(
        [
            total(grad_normed1 * scaled1),
            total(grad_normed1),
            total(grad_normed2 * scaled2),
            total(grad_normed2),
            total(three[0]),
            total(three[2]),
            total(grad_residual),
            total(grad_pre),
            total(grad_result),
        ]
    )
    return (output, grad_tokens, grads, sums)


def make_body(dp, tensor):

    def body(
        tokens,
        cotangent,
        block_patches,
        qkv,
        out,
        up,
        down,
        vectors,
        momentum,
        target_qkv,
        target_out,
        target_up,
        target_down,
        target_vectors,
    ):
        patches = block_patches[lax.axis_index("tensor")]
        blocks = gather_blocks(pack_shards(qkv, out, up, down), dp, tensor)
        output, grad_tokens, grads, sums = local_layer(tokens, cotangent, patches, blocks, vectors)
        grads = scatter_blocks(grads, dp, tensor).astype(F32)
        sums = lax.psum(sums, BOTH)
        w = qkv.shape[2]
        rate = momentum[0]

        def average(target, online):
            return rate * target + (1.0 - rate) * online.astype(F32)

        return (
            output,
            grad_tokens,
            jnp.stack([grads[0][:, i * w : (i + 1) * w] for i in range(3)]),
            grads[0][:, 3 * w :].T,
            grads[1],
            grads[2].T,
            sums,
            average(target_qkv, qkv),
            average(target_out, out),
            average(target_up, up),
            average(target_down, down),
            average(target_vectors, vectors),
        )

    return body


def solution(mesh):
    rows, matrices = (
        P(BOTH, None),
        (P(None, "dp", "tensor"), P("tensor", "dp"), P("dp", "tensor"), P("tensor", "dp")),
    )
    return jax.shard_map(
        make_body(mesh.shape["dp"], mesh.shape["tensor"]),
        mesh=mesh,
        in_specs=(rows, rows, P("dp")) + matrices + (P(), P()) + matrices + (P(),),
        out_specs=(rows, rows) + matrices + (P(),) + matrices + (P(),),
        check_vma=False,
    )
```

profile of v0, /device:TPU:0, one launch (start us, length us, event | category | flops | bytes accessed | tf_op | source)
XLA Modules:
  0.0 541.5 jit_solution(5149204099893250085)
XLA Ops:
  17.3 100.2 %all-gather.3.cloned.1.call-done = bf16[96,96,768]{2,1,0:T(8,128)(2,1)} async-done(((bf16[3,96,768]{2,1,0:T(8,128)(2,1)}), bf16[96,96,768]{2,1,0:T(8,128)(2,1)}) %all-gather.3.cloned.1.call-update) | async-done | bytes 14155792 | tf_op jit(solution)/shard_map/all_gather | solution.py:47
  117.5 5.9 %fusion.70 = (bf16[1,4,8,96,768]{4,3,0,1,2:T(8,128)(2,1)S(1)}, bf16[1,4,8,96,768]{4,3,0,1,2:T(8,128)(2,1)S(1)}, bf16[1,4,8,96,768]{4,3,0,1,2:T(8,128)(2,1)S(1)}) fusion(bf16[3,4,8,96,768]{4,3,0,1,2:T(8,128)(2,1)} %bitcast.155), kind=kLoop, calls=%fused_computation.137 | loop fusion | bytes 28311552 | tf_op jit(solution)/shard_map/slice | solution.py:70
  126.1 5.8 %fusion.17 = f32[784,4,576]{2,0,1:T(8,128)} fusion(bf16[4,768,768]{2,1,0:T(8,128)(2,1)S(1)} %bitcast.158, bf16[784,768]{1,0:T(8,128)(2,1)S(1)} %copy-done.2, f32[768]{0:T(1024)S(1)} %get-tuple-element.92, f32[768]{0:T(1024)S(1)} %get-tuple-element.93, f32[784]{0:T(1024)S(1)} %add_rsqrt_fusion.1, f32[784]{0:T(1024)S(1)} %broadcast_multiply_fusion.5), kind=kOutput, calls=%fused_computation.31 | convolution fusion | flops 2778144768 | bytes 12378112 | tf_op jit(solution)/shard_map/rd,tdc->rtc/dot_general | solution.py:75
  134.8 6.1 %fusion.71 = (f32[784,4,192]{2,0,1:T(8,128)}, f32[784,4,192]{2,0,1:T(8,128)}) fusion(f32[784,4,576]{2,0,1:T(8,128)} %fusion.17), kind=kLoop, calls=%fused_computation.138 | loop fusion | bytes 9633792 | tf_op jit(solution)/shard_map/slice | solution.py:76
  154.7 19.0 %fusion.73 = (f32[12,784]{1,0:T(8,128)S(1)}, f32[12,784,784]{1,2,0:T(8,128)}) fusion(pred[784,784]{0,1:T(8,128)(4,1)S(1)} %broadcast_compare_fusion, bf16[784,12,64]{0,2,1:T(8,128)(2,1)} %bitcast.161, f32[784,12,64]{0,2,1:T(8,128)S(1)} %bitcast.152, f32[12,64]{1,0:T(8,128)S(1)} %add.137), kind=kOutput, calls=%fused_computation.140 | convolution fusion | flops 974820096 | bytes 33771520 | tf_op jit(solution)/shard_map/sub | solution.py:83
  173.7 14.8 %fusion.42 = bf16[12,64,784]{2,1,0:T(8,128)(2,1)S(1)} fusion(f32[784,12,64]{0,2,1:T(8,128)} %bitcast.175, f32[12,64]{1,0:T(8,128)S(1)} %add.133, f32[12,784,784]{1,2,0:T(8,128)} %get-tuple-element.95, f32[12,784]{1,0:T(8,128)S(1)} %get-tuple-element.94), kind=kOutput, calls=%fused_computation.77 | convolution fusion | flops 960669696 | bytes 33156864 | tf_op jit(solution)/shard_map/hqk,khd->qhd/dot_general | solution.py:86
  193.3 6.2 %multiply_convert_fusion.1 = (bf16[784,4,768]{2,0,1:T(8,128)(2,1)}, f32[784,4,768]{2,0,1:T(8,128)S(1)}) fusion(f32[4,768]{1,0:T(4,128)S(1)} %slice.130, bf16[4,768,768]{2,1,0:T(8,128)(2,1)S(1)} %bitcast.173, f32[784,768]{1,0:T(8,128)S(1)} %get-tuple-element.97, f32[768]{0:T(1024)S(1)} %get-tuple-element.87, f32[768]{0:T(1024)S(1)} %get-tuple-element.88, ...), kind=kOutput, calls=%fused_computation.19 | convolution fusion | flops 3716837376 | bytes 21602432 | tf_op jit(solution)/shard_map/rd,tdf->rtf/dot_general | solution.py:92
  199.6 9.4 %convert_reduce_fusion = (f32[4,768]{1,0:T(4,128)}, bf16[784,4,768]{2,0,1:T(8,128)(2,1)S(1)}) fusion(f32[784,4,768]{2,0,1:T(8,128)S(1)} %get-tuple-element.99, f32[4,768]{1,0:T(4,128)S(1)} %slice.130, bf16[4,768,768]{2,1,0:T(8,128)(2,1)S(1)} %bitcast.170, bf16[784,768]{1,0:T(8,128)(2,1)S(1)} %copy-done.16), kind=kOutput, calls=%fused_computation.18 | convolution fusion | flops 3730682880 | bytes 20398080 | tf_op jit(solution)/shard_map/rd,tdf->rtf/dot_general | solution.py:99
  209.0 6.3 %fusion.37 = (f32[768]{0:T(1024)}, f32[784]{0:T(1024)S(1)}, f32[784]{0:T(1024)S(1)}, f32[768]{0:T(1024)}, f32[784,768,1]{1,0,2:T(8,128)}) fusion(f32[784,768]{1,0:T(8,128)S(1)} %get-tuple-element.97, f32[784]{0:T(1024)S(1)} %add_rsqrt_fusion, f32[784]{0:T(1024)S(1)} %broadcast_multiply_fusion.4, f32[768]{0:T(1024)S(1)} %get-tuple-element.88, ...), kind=kOutput, calls=%fused_computation.67 | convolution fusion | flops 3704792064 | bytes 14374144 | tf_op jit(solution)/shard_map/rtf,tdf->rd/dot_general | solution.py:103
  215.3 7.4 %convolution_convert_fusion.1 = bf16[4,768,768]{1,2,0:T(8,128)(2,1)} fusion(bf16[784,4,768]{2,0,1:T(8,128)(2,1)S(1)} %get-tuple-element.109, f32[784,768]{1,0:T(8,128)S(1)} %get-tuple-element.97, f32[768]{0:T(1024)S(1)} %get-tuple-element.87, f32[768]{0:T(1024)S(1)} %get-tuple-element.88, f32[784]{0:T(1024)S(1)} %add_rsqrt_fusion, ...), kind=kOutput, calls=%fused_computation.39 | convolution fusion | flops 3704745984 | bytes 11956352 | tf_op jit(solution)/shard_map/rd,rtf->tdf/dot_general | solution.py:102
  233.8 15.6 %convert_reduce_fusion.3 = (f32[12,64]{1,0:T(8,128)}, bf16[12,64,784]{2,1,0:T(8,128)(2,1)}) fusion(bf16[784,12,64]{0,2,1:T(8,128)(2,1)} %bitcast.179, f32[12,784,784]{1,2,0:T(8,128)} %get-tuple-element.95, f32[12,784]{1,0:T(8,128)S(1)} %get-tuple-element.94), kind=kOutput, calls=%fused_computation.46 | convolution fusion | flops 960668928 | bytes 31952640 | tf_op jit(solution)/shard_map/hqk,qhd->khd/dot_general | solution.py:110
  249.4 25.2 %multiply_reduce_fusion = (f32[12,784]{1,0:T(8,128)S(1)}, f32[12,784,784]{1,2,0:T(8,128)}) fusion(f32[12,784,784]{1,2,0:T(8,128)} %get-tuple-element.95, f32[12,784]{1,0:T(8,128)S(1)} %get-tuple-element.94, bf16[784,12,64]{0,2,1:T(8,128)(2,1)} %bitcast.180, f32[784,12,64]{0,2,1:T(8,128)S(1)} %bitcast.176, f32[12,64]{1,0:T(8,128)S(1)} %add.133), kind=kOutput, calls=%fused_computation.2 | convolution fusion | flops 967434048 | bytes 62697984 | tf_op jit(solution)/shard_map/qhd,khd->hqk/dot_general | solution.py:111
  274.6 27.9 %multiply_convert_fusion = bf16[12,784,784]{1,2,0:T(8,128)(2,1)} fusion(f32[12,784,784]{1,2,0:T(8,128)} %get-tuple-element.102, f32[12,784]{1,0:T(8,128)S(1)} %get-tuple-element.101, f32[12,784,784]{1,2,0:T(8,128)} %get-tuple-element.95, f32[12,784]{1,0:T(8,128)S(1)} %get-tuple-element.94), kind=kLoop, calls=%fused_computation.1 | loop fusion | flops 29503488 | bytes 73833984 | tf_op jit(solution)/shard_map/convert_element_type | solution.py:112
  302.5 10.1 %multiply_convert_fusion.2 = bf16[12,64,784]{2,1,0:T(8,128)(2,1)} fusion(bf16[12,784,784]{1,2,0:T(8,128)(2,1)} %multiply_convert_fusion, f32[784,12,64]{0,2,1:T(8,128)S(1)} %bitcast.153, f32[12,64]{1,0:T(8,128)S(1)} %copy-done.26), kind=kOutput, calls=%fused_computation.48 | convolution fusion | flops 946520064 | bytes 18367488 | tf_op jit(solution)/shard_map/hqk,qhd->khd/dot_general | solution.py:116
  312.7 10.8 %convert_reduce_fusion.4 = (f32[12,64]{1,0:T(8,128)}, bf16[12,64,784]{2,1,0:T(8,128)(2,1)}) fusion(bf16[784,12,64]{0,2,1:T(8,128)(2,1)S(1)} %bitcast.162, bf16[12,784,784]{1,2,0:T(8,128)(2,1)} %multiply_convert_fusion), kind=kOutput, calls=%fused_computation.47 | convolution fusion | flops 946519296 | bytes 17163264 | tf_op jit(solution)/shard_map/hqk,khd->qhd/dot_general | solution.py:115
  323.5 9.2 %convolution_convert_fusion = bf16[4,768,768]{1,2,0:T(8,128)(2,1)} fusion(bf16[784,4,768]{2,0,1:T(8,128)(2,1)} %get-tuple-element.98, bf16[784,768]{1,0:T(8,128)(2,1)S(1)} %copy-done.17), kind=kOutput, calls=%fused_computation.38 | convolution fusion | flops 3701735424 | bytes 10739712 | tf_op jit(solution)/shard_map/rd,rtf->tdf/dot_general | solution.py:101
  341.4 8.5 %convert_bitcast_fusion = bf16[4,768,576]{1,2,0:T(8,128)(2,1)} fusion(bf16[784,4,192]{2,0,1:T(8,128)(2,1)S(1)} %copy-done.14, bf16[784,4,192]{2,0,1:T(8,128)(2,1)} %copy.91, bf16[784,4,192]{2,0,1:T(8,128)(2,1)} %copy.90, bf16[784,768]{1,0:T(8,128)(2,1)S(1)} %copy-done.4, f32[768]{0:T(1024)S(1)} %copy-done.40, f32[768]{0:T(1024)S(1)} %copy-done.32, ...), kind=kOutput, calls=%fused_computation.30 | convolution fusion | flops 2790752256 | bytes 8368256 | tf_op jit(solution)/shard_map/rd,rtc->tdc/dot_general | solution.py:119
  350.0 6.1 %copy.93 = bf16[4,768,576]{2,1,0:T(8,128)(2,1)} copy(bf16[4,768,576]{1,2,0:T(8,128)(2,1)} %convert_bitcast_fusion) | data formatting | bytes 7077888 | tf_op jit(solution)/shard_map/rd,rtc->tdc/transpose | solution.py:119
  356.0 7.7 %maximum_bitcast_fusion = bf16[8,4,3,96,768]{4,3,0,1,2:T(8,128)(2,1)S(1)} fusion(bf16[1,4,8,96,768]{4,3,2,1,0:T(8,128)(2,1)} %bitcast.166, bf16[1,4,8,96,768]{4,3,2,1,0:T(8,128)(2,1)} %bitcast.165, bf16[1,4,8,96,192]{4,3,2,1,0:T(8,128)(2,1)S(1)} %bitcast.164, bf16[1,4,8,96,576]{4,3,2,1,0:T(8,128)(2,1)} %bitcast.154), kind=kLoop, calls=%fused_computation.11 | loop fusion | flops 56623104 | bytes 28311552 | tf_op jit(solution)/shard_map/transpose | solution.py:56
  363.7 6.0 %copy.95 = bf16[8,4,3,96,768]{4,3,2,1,0:T(8,128)(2,1)} copy(bf16[8,4,3,96,768]{4,3,0,1,2:T(8,128)(2,1)S(1)} %maximum_bitcast_fusion) | data formatting | bytes 28311552 | tf_op jit(solution)/shard_map/transpose | solution.py:56
  379.3 8.7 %fusion.34 = (f32[768]{0:T(1024)S(1)}, f32[784]{0:T(1024)S(1)}, f32[784]{0:T(1024)S(1)}, f32[768]{0:T(1024)S(1)}, f32[784,768,1]{1,0,2:T(8,128)}) fusion(bf16[784,768]{1,0:T(8,128)(2,1)S(1)} %copy-done.4, f32[784]{0:T(1024)} %copy-done.33, f32[784]{0:T(1024)S(1)} %copy-done.28, f32[768]{0:T(1024)S(1)} %copy-done.32, bf16[4,768,768]{2,1,0:T(8,128)(2,1)} %bitcast.160, ...), kind=kOutput, calls=%fused_computation.59 | convolution fusion | flops 2791388160 | bytes 11983040 | tf_op jit(solution)/shard_map/rtc,tdc->rd/dot_general | solution.py:120
  388.1 39.2 %psum.7 = f32[9216]{0:T(1024)} all-reduce(f32[9216]{0:T(1024)S(1)} %constant_dynamic-update-slice_fusion), channel_id=1, replica_groups=mesh['dp'=8,'tensor'=4] {'dp','tensor'}, use_global_device_ids=true, to_apply=%region_21.22 | all-reduce | flops 9216 | bytes 73728 | tf_op jit(solution)/shard_map/psum | solution.py:175
  431.2 8.8 %fusion.39 = bf16[784,768]{1,0:T(8,128)(2,1)} fusion(f32[784,768]{1,0:T(8,128)S(1)} %copy-done.9, bf16[784,4,768]{2,0,1:T(8,128)(2,1)} %get-tuple-element.98, bf16[4,768,768]{2,1,0:T(8,128)(2,1)} %bitcast.167, f32[768]{0:T(1024)S(1)} %copy-done.38), kind=kOutput, calls=%fused_computation.70 | convolution fusion | flops 3701182464 | bytes 13151232 | tf_op jit(solution)/shard_map/rtf,tdf->rd/dot_general | solution.py:97
  440.0 90.7 %reduce-scatter.2.cloned.1.call-done = bf16[1,3,96,768]{3,2,1,0:T(8,128)(2,1)} async-done(((bf16[32,3,96,768]{3,2,1,0:T(8,128)(2,1)}), bf16[1,3,96,768]{3,2,1,0:T(8,128)(2,1)}) %reduce-scatter.2.cloned.1.call-update) | async-done | bytes 442384 | tf_op jit(solution)/shard_map/reduce_scatter | solution.py:58
  (168 shorter events, 69.5 us)
Async XLA Ops:
  7.2 8.8 %copy-start.2 = (bf16[784,768]{1,0:T(8,128)(2,1)S(1)}, bf16[784,768]{1,0:T(8,128)(2,1)}, u32[]{:S(2)}) copy-start(bf16[784,768]{1,0:T(8,128)(2,1)} %param.14) | copy-start | bytes 3612676
  7.2 110.3 %all-gather.3.cloned.1.call-start = ((), (), s32[]{:S(2)}) async-start(), calls=%async_computation.2 | async-start | bytes 14598144 | tf_op jit(solution)/shard_map/all_gather | solution.py:47
  11.0 519.7 %reduce-scatter.2.cloned.1.call-start = ((), (), s32[]{:S(2)}) async-start(), calls=%async_computation.1 | async-start | bytes 14598144 | tf_op jit(solution)/shard_map/reduce_scatter | solution.py:58
  15.1 111.0 %copy-start.31 = (f32[768]{0:T(1024)}, f32[768]{0:T(1024)S(1)}, u32[]{:S(2)}) copy-start(f32[768]{0:T(1024)S(1)} %get-tuple-element.93) | copy-start | bytes 9220
  15.1 111.0 %copy-start.39 = (f32[768]{0:T(1024)}, f32[768]{0:T(1024)S(1)}, u32[]{:S(2)}) copy-start(f32[768]{0:T(1024)S(1)} %get-tuple-element.92) | copy-start | bytes 9220
  15.2 139.5 %copy-start.25 = (f32[12,64]{1,0:T(8,128)}, f32[12,64]{1,0:T(8,128)S(1)}, u32[]{:S(2)}) copy-start(f32[12,64]{1,0:T(8,128)S(1)} %add.137) | copy-start | bytes 9220
  16.3 109.8 %copy-start.27 = (f32[784]{0:T(1024)}, f32[784]{0:T(1024)S(1)}, u32[]{:S(2)}) copy-start(f32[784]{0:T(1024)S(1)} %broadcast_multiply_fusion.5) | copy-start | bytes 9412
  16.8 109.2 %copy-start.33 = (f32[784]{0:T(1024)}, f32[784]{0:T(1024)S(1)}, u32[]{:S(2)}) copy-start(f32[784]{0:T(1024)S(1)} %add_rsqrt_fusion.1) | copy-start | bytes 9412
  173.6 14.8 %copy-start.3 = (bf16[784,768]{1,0:T(8,128)(2,1)S(1)}, bf16[784,768]{1,0:T(8,128)(2,1)}, u32[]{:S(2)}) copy-start(bf16[784,768]{1,0:T(8,128)(2,1)} %param.14) | copy-start | bytes 3612676
  188.5 11.1 %slice-start = ((s8[4718592]{0:T(1024)(128)(4,1)}), s8[4194304]{0:T(1024)(128)(4,1)S(1)}, s32[]{:S(2)}) async-start(s8[4718592]{0:T(1024)(128)(4,1)} %bitcast.168), calls=%async_computation.3 | async-start | bytes 8388608
  192.8 22.5 %copy-start.7 = (f32[784,768]{1,0:T(8,128)}, f32[784,768]{1,0:T(8,128)S(1)}, u32[]{:S(2)}) copy-start(f32[784,768]{1,0:T(8,128)S(1)} %get-tuple-element.97) | copy-start | bytes 7225348
  233.8 15.6 %copy-start.13 = (f32[784,4,192]{0,2,1:T(8,128)S(1)}, f32[784,4,192]{0,2,1:T(8,128)}, u32[]{:S(2)}) copy-start(f32[784,4,192]{0,2,1:T(8,128)} %copy.80) | copy-start | bytes 7225348
  274.6 27.9 %copy-start.1 = (f32[784,4,192]{0,2,1:T(8,128)S(1)}, f32[784,4,192]{0,2,1:T(8,128)}, u32[]{:S(2)}) copy-start(f32[784,4,192]{0,2,1:T(8,128)} %copy-done) | copy-start | bytes 7225348
  274.6 27.9 %copy-start.26 = (f32[12,64]{1,0:T(8,128)S(1)}, f32[12,64]{1,0:T(8,128)}, u32[]{:S(2)}) copy-start(f32[12,64]{1,0:T(8,128)} %copy-done.25) | copy-start | bytes 9220
  302.5 10.1 %copy-start.11 = (bf16[784,4,192]{0,2,1:T(8,128)(2,1)S(1)}, bf16[784,4,192]{0,2,1:T(8,128)(2,1)}, u32[]{:S(2)}) copy-start(bf16[784,4,192]{0,2,1:T(8,128)(2,1)} %copy.82) | copy-start | bytes 3612676
  312.7 10.8 %copy-start.17 = (bf16[784,768]{1,0:T(8,128)(2,1)S(1)}, bf16[784,768]{1,0:T(8,128)(2,1)}, u32[]{:S(2)}) copy-start(bf16[784,768]{1,0:T(8,128)(2,1)} %param.15) | copy-start | bytes 3612676
  323.5 9.2 %copy-start.18 = (bf16[4,768,192]{1,2,0:T(8,128)(2,1)S(1)}, bf16[4,768,192]{1,2,0:T(8,128)(2,1)}, u32[]{:S(2)}) copy-start(bf16[4,768,192]{1,2,0:T(8,128)(2,1)} %fusion.48) | copy-start | bytes 3538948
  369.7 9.6 %copy-start.15 = (bf16[784,4,192]{2,0,1:T(8,128)(2,1)S(1)}, bf16[784,4,192]{2,0,1:T(8,128)(2,1)}, u32[]{:S(2)}) copy-start(bf16[784,4,192]{2,0,1:T(8,128)(2,1)} %copy.92) | copy-start | bytes 3612676
  379.3 8.7 %copy-start.30 = (f32[9216]{0:T(1024)S(1)}, f32[9216]{0:T(1024)}, u32[]{:S(2)}) copy-start(f32[9216]{0:T(1024)} %custom-call) | copy-start | bytes 110596
  379.3 8.8 %copy-start.42 = (f32[768]{0:T(1024)S(1)}, f32[768]{0:T(1024)}, u32[]{:S(2)}) copy-start(f32[768]{0:T(1024)} %get-tuple-element.60) | copy-start | bytes 9220
  379.3 8.8 %copy-start.41 = (f32[768]{0:T(1024)S(1)}, f32[768]{0:T(1024)}, u32[]{:S(2)}) copy-start(f32[768]{0:T(1024)} %get-tuple-element.66) | copy-start | bytes 9220
  379.3 8.8 %copy-start.37 = (f32[768]{0:T(1024)S(1)}, f32[768]{0:T(1024)}, u32[]{:S(2)}) copy-start(f32[768]{0:T(1024)} %get-tuple-element.68) | copy-start | bytes 9220
  379.3 8.8 %copy-start.36 = (f32[768]{0:T(1024)S(1)}, f32[768]{0:T(1024)}, u32[]{:S(2)}) copy-start(f32[768]{0:T(1024)} %get-tuple-element.75) | copy-start | bytes 9220
  379.3 48.1 %copy-start.35 = (f32[784]{0:T(1024)S(1)}, f32[784]{0:T(1024)}, u32[]{:S(2)}) copy-start(f32[784]{0:T(1024)} %copy-done.33) | copy-start | bytes 9412
  (27 other events, 117.8 us)
Sparse Core Ops, SparseCore 0:
  11.5 105.9 all-gather.2
  369.8 160.8 reduce-scatter.1
where the time goes:
time: 552 us; the launch traced here: 542 us
  waiting for transfers between devices  191 us (35%)
  matrix products  174 us (32%)
  local copies, waits for them, and re-layouts  64.2 us (12%)
  other arithmetic  56.6 us (10%)
  blocking collectives  39.2 us (7%)
  between operations  16.5 us (3%)
    all_gather x1, waiting for transfers between devices, gather_blocks(): every = lax.all_gather(shards, BOTH, axis=0)  100 us
    reduce_scatter x1, waiting for transfers between devices, scatter_blocks(): return lax.psum_scatter(pieces, BOTH, scatter_dimension=0, tiled=True)[0]  90.7 us
    psum x1, blocking collectives, body(): sums = lax.psum(sums, BOTH)  39.2 us
    convert_element_type x1, other arithmetic, local_layer(): (soft * (grad_soft - jnp.sum(soft * grad_soft, axis=-1, keepdims=True)))....  27.9 us
    dot_general x1, matrix products, local_layer(): jnp.einsum('qhd,khd->hqk', grad_att, value, preferred_element_type=F32)  25.2 us
    sub x1, matrix products, local_layer(): raised = jnp.exp(scores - jnp.max(scores, axis=-1, keepdims=True))  19 us
    dot_general x1, matrix products, local_layer(): jnp.einsum('hqk,qhd->khd', soft_low, grad_att, preferred_element_type=F32)  15.6 us
    dot_general x1, matrix products, local_layer(): jnp.einsum('hqk,khd->qhd', soft_low, value, preferred_element_type=F32)  14.8 us
  transfers between devices with their start and end apart: 2, of which 2 were waited for; matrix products, arithmetic and copies ran while one was open for 7% of the time, Pallas kernels for 0%

commit v1 on v0

--- a/solution.py
+++ b/solution.py
@@ -172,7 +172,8 @@
         blocks = gather_blocks(pack_shards(qkv, out, up, down), dp, tensor)
         output, grad_tokens, grads, sums = local_layer(tokens, cotangent, patches, blocks, vectors)
         grads = scatter_blocks(grads, dp, tensor).astype(F32)
-        sums = lax.psum(sums, BOTH)
+        shards_2 = lax.all_gather(sums, BOTH)
+        sums = jnp.sum(shards_2, axis=0)
         w = qkv.shape[2]
         rate = momentum[0]
 

time: 552 us -> 581 us (1.053)
  waiting for transfers between devices: 191 us -> 275 us
  blocking collectives: 39.2 us -> 0 us
    reduce_scatter x1, waiting for transfers between devices: 90.7 us -> 166 us  [scatter_blocks(): return lax.psum_scatter(pieces, BOTH, scatter_dimension=0, tiled=True)[0]]
    psum x1 -> x0, blocking collectives: 39.2 us -> none  [body(): sums = lax.psum(sums, BOTH)]
    all_gather x0 -> x1, waiting for transfers between devices: none -> 9.83 us  [body(): shards_2 = lax.all_gather(sums, BOTH)]
  transfers between devices with their start and end apart: 2 -> 3, of which waited for: 2 -> 3; matrix products, arithmetic and copies ran while one was open for 7% -> 9% of each run, Pallas kernels for 0% -> 0%
where the time goes in v1:
time: 581 us; the launch traced here: 574 us
  waiting for transfers between devices  275 us (47%)
  matrix products  170 us (29%)
  local copies, waits for them, and re-layouts  61.2 us (11%)
  other arithmetic  51.4 us (9%)
  between operations  16.1 us (3%)
    reduce_scatter x1, waiting for transfers between devices, scatter_blocks(): return lax.psum_scatter(pieces, BOTH, scatter_dimension=0, tiled=True)[0]  166 us
    all_gather x1, waiting for transfers between devices, gather_blocks(): every = lax.all_gather(shards, BOTH, axis=0)  99.3 us
    convert_element_type x1, other arithmetic, local_layer(): (soft * (grad_soft - jnp.sum(soft * grad_soft, axis=-1, keepdims=True)))....  27.9 us
    dot_general x1, matrix products, local_layer(): jnp.einsum('qhd,khd->hqk', grad_att, value, preferred_element_type=F32)  25.6 us
    sub x1, matrix products, local_layer(): raised = jnp.exp(scores - jnp.max(scores, axis=-1, keepdims=True))  18.8 us
    dot_general x1, matrix products, local_layer(): jnp.einsum('hqk,qhd->khd', soft_low, grad_att, preferred_element_type=F32)  15 us
    dot_general x1, matrix products, local_layer(): jnp.einsum('hqk,khd->qhd', soft_low, value, preferred_element_type=F32)  14.8 us
  transfers between devices with their start and end apart: 3, of which 3 were waited for; matrix products, arithmetic and copies ran while one was open for 9% of the time, Pallas kernels for 0%

profile of v1, /device:TPU:0, one launch (start us, length us, event | category | flops | bytes accessed | tf_op | source)
XLA Modules:
  0.0 573.8 jit_solution(10394894747638937004)
XLA Ops:
  18.2 99.3 %all-gather.5.cloned.1.call-done = bf16[96,96,768]{2,1,0:T(8,128)(2,1)} async-done(((bf16[3,96,768]{2,1,0:T(8,128)(2,1)}), bf16[96,96,768]{2,1,0:T(8,128)(2,1)}) %all-gather.5.cloned.1.call-update) | async-done | bytes 14155792 | tf_op jit(solution)/shard_map/all_gather | solution.py:47
  117.5 5.9 %fusion.70 = (bf16[1,4,8,96,768]{4,3,0,1,2:T(8,128)(2,1)S(1)}, bf16[1,4,8,96,768]{4,3,0,1,2:T(8,128)(2,1)S(1)}, bf16[1,4,8,96,768]{4,3,0,1,2:T(8,128)(2,1)S(1)}) fusion(bf16[3,4,8,96,768]{4,3,0,1,2:T(8,128)(2,1)} %bitcast.155), kind=kLoop, calls=%fused_computation.137 | loop fusion | bytes 28311552 | tf_op jit(solution)/shard_map/slice | solution.py:70
  124.5 5.8 %fusion.17 = f32[784,4,576]{2,0,1:T(8,128)} fusion(bf16[4,768,768]{2,1,0:T(8,128)(2,1)S(1)} %bitcast.158, bf16[784,768]{1,0:T(8,128)(2,1)S(1)} %copy-done.3, f32[768]{0:T(1024)S(1)} %get-tuple-element.104, f32[768]{0:T(1024)S(1)} %get-tuple-element.105, f32[784]{0:T(1024)S(1)} %add_rsqrt_fusion.1, f32[784]{0:T(1024)S(1)} %broadcast_multiply_fusion.5), kind=kOutput, calls=%fused_computation.31 | convolution fusion | flops 2778144768 | bytes 12378112 | tf_op jit(solution)/shard_map/rd,tdc->rtc/dot_general | solution.py:75
  133.3 6.0 %fusion.71 = (f32[784,4,192]{2,0,1:T(8,128)}, f32[784,4,192]{2,0,1:T(8,128)}) fusion(f32[784,4,576]{2,0,1:T(8,128)} %fusion.17), kind=kLoop, calls=%fused_computation.138 | loop fusion | bytes 9633792 | tf_op jit(solution)/shard_map/slice | solution.py:76
  154.6 18.8 %fusion.73 = (f32[12,784]{1,0:T(8,128)S(1)}, f32[12,784,784]{1,2,0:T(8,128)}) fusion(pred[784,784]{0,1:T(8,128)(4,1)S(1)} %copy-done.20, bf16[784,12,64]{0,2,1:T(8,128)(2,1)} %bitcast.161, f32[784,12,64]{0,2,1:T(8,128)S(1)} %bitcast.152, f32[12,64]{1,0:T(8,128)S(1)} %add.135), kind=kOutput, calls=%fused_computation.140 | convolution fusion | flops 974820096 | bytes 33771520 | tf_op jit(solution)/shard_map/sub | solution.py:83
  173.5 14.8 %fusion.42 = bf16[12,64,784]{2,1,0:T(8,128)(2,1)S(1)} fusion(f32[784,12,64]{0,2,1:T(8,128)} %bitcast.175, f32[12,64]{1,0:T(8,128)S(1)} %add.131, f32[12,784,784]{1,2,0:T(8,128)} %get-tuple-element.107, f32[12,784]{1,0:T(8,128)S(1)} %get-tuple-element.106), kind=kOutput, calls=%fused_computation.77 | convolution fusion | flops 960669696 | bytes 33156864 | tf_op jit(solution)/shard_map/hqk,khd->qhd/dot_general | solution.py:86
  192.8 6.5 %multiply_convert_fusion.1 = (bf16[784,4,768]{2,0,1:T(8,128)(2,1)}, f32[784,4,768]{2,0,1:T(8,128)S(1)}) fusion(f32[4,768]{1,0:T(4,128)S(1)} %slice.130, bf16[4,768,768]{2,1,0:T(8,128)(2,1)S(1)} %bitcast.173, f32[784,768]{1,0:T(8,128)S(1)} %get-tuple-element.109, f32[768]{0:T(1024)S(1)} %get-tuple-element.99, f32[768]{0:T(1024)S(1)} %get-tuple-element.100, ...), kind=kOutput, calls=%fused_computation.19 | convolution fusion | flops 3716837376 | bytes 21602432 | tf_op jit(solution)/shard_map/rd,tdf->rtf/dot_general | solution.py:92
  199.3 9.4 %convert_reduce_fusion = (f32[4,768]{1,0:T(4,128)}, bf16[784,4,768]{2,0,1:T(8,128)(2,1)S(1)}) fusion(f32[784,4,768]{2,0,1:T(8,128)S(1)} %get-tuple-element.111, f32[4,768]{1,0:T(4,128)S(1)} %slice.130, bf16[4,768,768]{2,1,0:T(8,128)(2,1)S(1)} %bitcast.170, bf16[784,768]{1,0:T(8,128)(2,1)S(1)} %copy-done.17), kind=kOutput, calls=%fused_computation.18 | convolution fusion | flops 3730682880 | bytes 20398080 | tf_op jit(solution)/shard_map/rd,tdf->rtf/dot_general | solution.py:99
  208.7 4.9 fusion.37
  220.6 15.0 %convert_reduce_fusion.3 = (f32[12,64]{1,0:T(8,128)S(1)}, bf16[12,64,784]{2,1,0:T(8,128)(2,1)}) fusion(bf16[784,12,64]{0,2,1:T(8,128)(2,1)} %bitcast.179, f32[12,784,784]{1,2,0:T(8,128)} %get-tuple-element.107, f32[12,784]{1,0:T(8,128)S(1)} %get-tuple-element.106), kind=kOutput, calls=%fused_computation.46 | convolution fusion | flops 960668928 | bytes 31952640 | tf_op jit(solution)/shard_map/hqk,qhd->khd/dot_general | solution.py:110
  235.6 25.6 %multiply_reduce_fusion = (f32[12,784]{1,0:T(8,128)S(1)}, f32[12,784,784]{1,2,0:T(8,128)}) fusion(f32[12,784,784]{1,2,0:T(8,128)} %get-tuple-element.107, f32[12,784]{1,0:T(8,128)S(1)} %get-tuple-element.106, bf16[784,12,64]{0,2,1:T(8,128)(2,1)} %bitcast.180, f32[784,12,64]{0,2,1:T(8,128)S(1)} %bitcast.176, f32[12,64]{1,0:T(8,128)S(1)} %add.131), kind=kOutput, calls=%fused_computation.2 | convolution fusion | flops 967434048 | bytes 62697984 | tf_op jit(solution)/shard_map/qhd,khd->hqk/dot_general | solution.py:111
  261.3 27.9 %multiply_convert_fusion = bf16[12,784,784]{1,2,0:T(8,128)(2,1)} fusion(f32[12,784,784]{1,2,0:T(8,128)} %get-tuple-element.114, f32[12,784]{1,0:T(8,128)S(1)} %get-tuple-element.113, f32[12,784,784]{1,2,0:T(8,128)} %get-tuple-element.107, f32[12,784]{1,0:T(8,128)S(1)} %get-tuple-element.106), kind=kLoop, calls=%fused_computation.1 | loop fusion | flops 29503488 | bytes 73833984 | tf_op jit(solution)/shard_map/convert_element_type | solution.py:112
  289.1 10.0 %multiply_convert_fusion.2 = bf16[12,64,784]{2,1,0:T(8,128)(2,1)} fusion(bf16[12,784,784]{1,2,0:T(8,128)(2,1)} %multiply_convert_fusion, f32[784,12,64]{0,2,1:T(8,128)S(1)} %bitcast.153, f32[12,64]{1,0:T(8,128)S(1)} %copy-done.30), kind=kOutput, calls=%fused_computation.48 | convolution fusion | flops 946520064 | bytes 18367488 | tf_op jit(solution)/shard_map/hqk,qhd->khd/dot_general | solution.py:116
  299.1 10.1 %convert_reduce_fusion.4 = (f32[12,64]{1,0:T(8,128)S(1)}, bf16[12,64,784]{2,1,0:T(8,128)(2,1)}) fusion(bf16[784,12,64]{0,2,1:T(8,128)(2,1)S(1)} %bitcast.162, bf16[12,784,784]{1,2,0:T(8,128)(2,1)} %multiply_convert_fusion), kind=kOutput, calls=%fused_computation.47 | convolution fusion | flops 946519296 | bytes 17163264 | tf_op jit(solution)/shard_map/hqk,khd->qhd/dot_general | solution.py:115
  316.4 8.4 %fusion.34 = (f32[768]{0:T(1024)S(1)}, f32[784]{0:T(1024)S(1)}, f32[784]{0:T(1024)S(1)}, f32[768]{0:T(1024)S(1)}, f32[784,768,1]{1,0,2:T(8,128)}) fusion(bf16[784,768]{1,0:T(8,128)(2,1)S(1)} %copy-done.5, f32[784]{0:T(1024)S(1)} %copy-done.44, f32[784]{0:T(1024)S(1)} %copy-done.33, f32[768]{0:T(1024)S(1)} %copy-done.40, bf16[4,768,768]{2,1,0:T(8,128)(2,1)} %bitcast.160, ...), kind=kOutput, calls=%fused_computation.59 | convolution fusion | flops 2791388160 | bytes 11982080 | tf_op jit(solution)/shard_map/rtc,tdc->rd/dot_general | solution.py:120
  324.8 6.8 %convert_bitcast_fusion = bf16[4,768,576]{1,2,0:T(8,128)(2,1)} fusion(bf16[784,4,192]{2,0,1:T(8,128)(2,1)S(1)} %copy-done.14, bf16[784,4,192]{2,0,1:T(8,128)(2,1)S(1)} %copy-done.15, bf16[784,4,192]{2,0,1:T(8,128)(2,1)S(1)} %copy-done.16, bf16[784,768]{1,0:T(8,128)(2,1)S(1)} %copy-done.5, f32[768]{0:T(1024)S(1)} %copy-done.54, f32[768]{0:T(1024)S(1)} %copy-done.40, ...), kind=kOutput, calls=%fused_computation.30 | convolution fusion | flops 2790752256 | bytes 8368256 | tf_op jit(solution)/shard_map/rd,rtc->tdc/dot_general | solution.py:119
  331.6 9.1 %convolution_convert_fusion = bf16[4,768,768]{1,2,0:T(8,128)(2,1)} fusion(bf16[784,4,768]{2,0,1:T(8,128)(2,1)} %get-tuple-element.110, bf16[784,768]{1,0:T(8,128)(2,1)S(1)} %copy-done.18), kind=kOutput, calls=%fused_computation.38 | convolution fusion | flops 3701735424 | bytes 10739712 | tf_op jit(solution)/shard_map/rd,rtf->tdf/dot_general | solution.py:101
  343.5 5.9 %copy.113 = bf16[4,768,576]{2,1,0:T(8,128)(2,1)} copy(bf16[4,768,576]{1,2,0:T(8,128)(2,1)} %convert_bitcast_fusion) | data formatting | bytes 7077888 | tf_op jit(solution)/shard_map/rd,rtc->tdc/transpose | solution.py:119
  349.4 8.5 %convolution_convert_fusion.1 = bf16[4,768,768]{1,2,0:T(8,128)(2,1)S(1)} fusion(bf16[784,4,768]{2,0,1:T(8,128)(2,1)} %copy-done.57, f32[784,768]{1,0:T(8,128)} %copy-done.9, f32[768]{0:T(1024)S(1)} %copy-done.52, f32[768]{0:T(1024)S(1)} %copy-done.42, f32[784]{0:T(1024)S(1)} %copy-done.46, f32[784]{0:T(1024)S(1)} %copy-done.35), kind=kOutput, calls=%fused_computation.39 | convolution fusion | flops 3704745984 | bytes 11956352 | tf_op jit(solution)/shard_map/rd,rtf->tdf/dot_general | solution.py:102
  357.9 5.8 %maximum_bitcast_fusion = bf16[8,4,3,96,768]{4,3,0,1,2:T(8,128)(2,1)S(1)} fusion(bf16[1,4,8,96,768]{4,3,2,1,0:T(8,128)(2,1)} %bitcast.165, bf16[1,4,8,96,768]{4,3,2,1,0:T(8,128)(2,1)S(1)} %bitcast.166, bf16[1,4,8,96,192]{4,3,2,1,0:T(8,128)(2,1)S(1)} %bitcast.164, bf16[1,4,8,96,576]{4,3,2,1,0:T(8,128)(2,1)S(1)} %bitcast.154), kind=kLoop, calls=%fused_computation.11 | loop fusion | flops 56623104 | bytes 28311552 | tf_op jit(solution)/shard_map/transpose | solution.py:56
  363.8 5.6 copy.115
  377.2 8.8 %fusion.39 = bf16[784,768]{1,0:T(8,128)(2,1)} fusion(f32[784,768]{1,0:T(8,128)S(1)} %copy-done.10, bf16[784,4,768]{2,0,1:T(8,128)(2,1)} %get-tuple-element.110, bf16[4,768,768]{2,1,0:T(8,128)(2,1)} %bitcast.167, f32[768]{0:T(1024)S(1)} %copy-done.50), kind=kOutput, calls=%fused_computation.70 | convolution fusion | flops 3701182464 | bytes 13151232 | tf_op jit(solution)/shard_map/rtf,tdf->rd/dot_general | solution.py:97
  385.9 9.8 %all-gather.7.cloned.1.call-done = f32[294912]{0:T(1024)} async-done(((f32[9216]{0:T(1024)}), f32[294912]{0:T(1024)}) %all-gather.7.cloned.1.call-update) | async-done | bytes 1179664 | tf_op jit(solution)/shard_map/all_gather | solution.py:175
  397.9 165.6 %reduce-scatter.2.cloned.1.call-done = bf16[1,3,96,768]{3,2,1,0:T(8,128)(2,1)} async-done(((bf16[32,3,96,768]{3,2,1,0:T(8,128)(2,1)}), bf16[1,3,96,768]{3,2,1,0:T(8,128)(2,1)}) %reduce-scatter.2.cloned.1.call-update) | async-done | bytes 442384 | tf_op jit(solution)/shard_map/reduce_scatter | solution.py:58
  (198 shorter events, 63.4 us)
Async XLA Ops:
  7.2 8.9 %copy-start.3 = (bf16[784,768]{1,0:T(8,128)(2,1)S(1)}, bf16[784,768]{1,0:T(8,128)(2,1)}, u32[]{:S(2)}) copy-start(bf16[784,768]{1,0:T(8,128)(2,1)} %param.14) | copy-start | bytes 3612676
  7.2 110.3 %all-gather.5.cloned.1.call-start = ((), (), s32[]{:S(2)}) async-start(), calls=%async_computation.2 | async-start | bytes 14598144 | tf_op jit(solution)/shard_map/all_gather | solution.py:47
  11.0 384.7 %all-gather.7.cloned.1.call-start = ((), (), s32[]{:S(2)}) async-start(), calls=%async_computation.3 | async-start | bytes 1216512 | tf_op jit(solution)/shard_map/all_gather | solution.py:175
  15.1 109.3 %copy-start.39 = (f32[768]{0:T(1024)}, f32[768]{0:T(1024)S(1)}, u32[]{:S(2)}) copy-start(f32[768]{0:T(1024)S(1)} %get-tuple-element.105) | copy-start | bytes 9220
  15.1 109.3 %copy-start.53 = (f32[768]{0:T(1024)}, f32[768]{0:T(1024)S(1)}, u32[]{:S(2)}) copy-start(f32[768]{0:T(1024)S(1)} %get-tuple-element.104) | copy-start | bytes 9220
  15.1 177.6 %copy-start.51 = (f32[768]{0:T(1024)}, f32[768]{0:T(1024)S(1)}, u32[]{:S(2)}) copy-start(f32[768]{0:T(1024)S(1)} %get-tuple-element.99) | copy-start | bytes 9220
  15.1 198.5 %copy-start.41 = (f32[768]{0:T(1024)}, f32[768]{0:T(1024)S(1)}, u32[]{:S(2)}) copy-start(f32[768]{0:T(1024)S(1)} %get-tuple-element.100) | copy-start | bytes 9220
  15.2 139.4 %copy-start.29 = (f32[12,64]{1,0:T(8,128)}, f32[12,64]{1,0:T(8,128)S(1)}, u32[]{:S(2)}) copy-start(f32[12,64]{1,0:T(8,128)S(1)} %add.135) | copy-start | bytes 9220
  16.3 108.2 %copy-start.32 = (f32[784]{0:T(1024)}, f32[784]{0:T(1024)S(1)}, u32[]{:S(2)}) copy-start(f32[784]{0:T(1024)S(1)} %broadcast_multiply_fusion.5) | copy-start | bytes 9412
  16.8 107.6 %copy-start.43 = (f32[784]{0:T(1024)}, f32[784]{0:T(1024)S(1)}, u32[]{:S(2)}) copy-start(f32[784]{0:T(1024)S(1)} %add_rsqrt_fusion.1) | copy-start | bytes 9412
  173.5 14.8 %copy-start.4 = (bf16[784,768]{1,0:T(8,128)(2,1)S(1)}, bf16[784,768]{1,0:T(8,128)(2,1)}, u32[]{:S(2)}) copy-start(bf16[784,768]{1,0:T(8,128)(2,1)} %param.14) | copy-start | bytes 3612676
  188.3 11.0 %slice-start = ((s8[4718592]{0:T(1024)(128)(4,1)}), s8[4194304]{0:T(1024)(128)(4,1)S(1)}, s32[]{:S(2)}) async-start(s8[4718592]{0:T(1024)(128)(4,1)} %bitcast.168), calls=%async_computation.4 | async-start | bytes 8388608
  192.2 21.4 %copy-start.9 = (f32[784,768]{1,0:T(8,128)}, f32[784,768]{1,0:T(8,128)S(1)}, u32[]{:S(2)}) copy-start(f32[784,768]{1,0:T(8,128)S(1)} %get-tuple-element.109) | copy-start | bytes 7225348
  192.2 21.4 %copy-start.34 = (f32[784]{0:T(1024)}, f32[784]{0:T(1024)S(1)}, u32[]{:S(2)}) copy-start(f32[784]{0:T(1024)S(1)} %broadcast_multiply_fusion.4) | copy-start | bytes 9412
  192.7 20.9 %copy-start.45 = (f32[784]{0:T(1024)}, f32[784]{0:T(1024)S(1)}, u32[]{:S(2)}) copy-start(f32[784]{0:T(1024)S(1)} %add_rsqrt_fusion) | copy-start | bytes 9412
  220.6 15.0 %copy-start.13 = (f32[784,4,192]{0,2,1:T(8,128)S(1)}, f32[784,4,192]{0,2,1:T(8,128)}, u32[]{:S(2)}) copy-start(f32[784,4,192]{0,2,1:T(8,128)} %copy.100) | copy-start | bytes 7225348
  261.3 27.9 %copy-start.1 = (f32[784,4,192]{0,2,1:T(8,128)S(1)}, f32[784,4,192]{0,2,1:T(8,128)}, u32[]{:S(2)}) copy-start(f32[784,4,192]{0,2,1:T(8,128)} %copy-done) | copy-start | bytes 7225348
  261.3 27.9 %copy-start.30 = (f32[12,64]{1,0:T(8,128)S(1)}, f32[12,64]{1,0:T(8,128)}, u32[]{:S(2)}) copy-start(f32[12,64]{1,0:T(8,128)} %copy-done.29) | copy-start | bytes 9220
  289.1 10.0 %copy-start.12 = (bf16[784,4,192]{0,2,1:T(8,128)(2,1)S(1)}, bf16[784,4,192]{0,2,1:T(8,128)(2,1)}, u32[]{:S(2)}) copy-start(bf16[784,4,192]{0,2,1:T(8,128)(2,1)} %copy.102) | copy-start | bytes 3612676
  316.4 8.4 %copy-start.15 = (bf16[784,4,192]{2,0,1:T(8,128)(2,1)S(1)}, bf16[784,4,192]{2,0,1:T(8,128)(2,1)}, u32[]{:S(2)}) copy-start(bf16[784,4,192]{2,0,1:T(8,128)(2,1)} %copy.111) | copy-start | bytes 3612676
  316.4 8.4 %copy-start.16 = (bf16[784,4,192]{2,0,1:T(8,128)(2,1)S(1)}, bf16[784,4,192]{2,0,1:T(8,128)(2,1)}, u32[]{:S(2)}) copy-start(bf16[784,4,192]{2,0,1:T(8,128)(2,1)} %copy.110) | copy-start | bytes 3612676
  331.6 9.2 %copy-start.49 = (f32[4,768]{1,0:T(4,128)S(1)}, f32[4,768]{1,0:T(4,128)}, u32[]{:S(2)}) copy-start(f32[4,768]{1,0:T(4,128)} %get-tuple-element.120) | copy-start | bytes 36868
  343.4 220.1 %reduce-scatter.2.cloned.1.call-start = ((), (), s32[]{:S(2)}) async-start(), calls=%async_computation.1 | async-start | bytes 14598144 | tf_op jit(solution)/shard_map/reduce_scatter | solution.py:58
  349.4 8.5 %copy-start.2 = (bf16[4,768,576]{2,1,0:T(8,128)(2,1)S(1)}, bf16[4,768,576]{2,1,0:T(8,128)(2,1)}, u32[]{:S(2)}) copy-start(bf16[4,768,576]{2,1,0:T(8,128)(2,1)} %copy.113) | copy-start | bytes 10616836
  (41 other events, 153.6 us)
Sparse Core Ops, SparseCore 0:
  11.5 105.9 all-gather.4
  343.5 52.2 all-gather.6
  401.8 161.7 reduce-scatter.1
